TPU v7x, 256 devices: a whole 4x4x8 slice. The times are simulated.
256 devices in a mesh: pw: 64 (over y_lo, z, x), atom: 4 (over y_hi, core).
Axes of the slice: x: 4, y: 4 (y_hi: 2, y_lo: 2; y = y_hi * 2 + y_lo), z: 8, core: 2. Of those that a mesh axis runs over, the one named last changes fastest.
Arguments:
- bands_in: float32 [2, 8, 32768], P(None, None, 'pw'), may hold values from -6 to 6
- template: bfloat16 [2, 64, 32768], P(None, None, 'pw'), may hold values from -0.03125 to 0.03125
- potential: bfloat16 [1024, 8192], P(('pw', 'atom')), may hold values from -0.5 to 0.5
- miller: int32 [3, 32768], P(None, 'pw'), may hold values from -32 to 32, as said below
- positions: float32 [3, 1024], replicated, may hold values from 0 to 1
- species: int32 [1024], replicated, may hold values from 0 to 1
- atom_order: int32 [1024], replicated, may hold values from 0 to 1023, each once
- reciprocal: float32 [3], replicated, may hold values from 0.03 to 0.1
Outputs:
- applied_once: float32 [2, 8, 32768], P(None, None, 'pw')
- applied_twice: float32 [2, 8, 32768], P(None, None, 'pw')
Inputs may be any that keep to these rules, and one draw needn't show every extreme that they name: `atom_order`: each atom stands in exactly one slot. `miller`: no two plane waves have the same triple of Miller indices; the triples (-32, -32, -32) and (32, 32, 32) are always among them.
All inputs are finite; a program needn't handle non-finite values.
Results may differ from a plain program's by a relative error of at most 0.005.
Values may be sent and summed in bfloat16 or wider, within the bound.
No kernel may reach another device: no remote copies, remote signals or barrier semaphores. Data moves between devices by JAX's collectives and lax.ppermute only.
A program may use at most 64 MiB of HBM per device.

v0:
```python
import math
import jax
import jax.numpy as jnp
from jax import lax
from jax.sharding import PartitionSpec as P

full_turn = 2.0 * math.pi


def phases(miller_real, centres):
    angles = full_turn * (
        centres[0][:, None] * miller_real[0][None, :]
        + centres[1][:, None] * miller_real[1][None, :]
        + centres[2][:, None] * miller_real[2][None, :]
    )
    return (jnp.cos(angles), jnp.sin(angles))


def project_block(template_flat, fields, cos_part, sin_part, chosen):
    band_count = fields.shape[1]
    real_wave = cos_part[:, None, :] * fields[0][None] - sin_part[:, None, :] * fields[1][None]
    imag_wave = sin_part[:, None, :] * fields[0][None] + cos_part[:, None, :] * fields[1][None]
    stacked = jnp.stack([real_wave, imag_wave], axis=1).astype(jnp.bfloat16)
    atom_count = stacked.shape[0]
    flattened = stacked.reshape(atom_count * 2 * band_count, stacked.shape[3])
    correlations = lax.dot_general(
        template_flat, flattened, (((1,), (1,)), ((), ())), preferred_element_type=jnp.float32
    )
    species_count = chosen.shape[1]
    harmonics = template_flat.shape[0] // species_count
    correlations = correlations.reshape(species_count, harmonics, atom_count, 2, band_count)
    accumulated = jnp.zeros((harmonics, atom_count, 2, band_count), jnp.float32)
    for species_id in range(species_count):
        accumulated = (
            accumulated + chosen[:, species_id][None, :, None, None] * correlations[species_id]
        )
    return jnp.transpose(accumulated, (1, 2, 0, 3))


def product(matrices, vectors):
    return jnp.einsum("alm,amb->alb", matrices, vectors, precision=lax.Precision.HIGHEST)


def apply_potential(potential, coeffs):
    atom_count = coeffs.shape[0]
    harmonics = coeffs.shape[2]
    matrices = potential.astype(jnp.float32).reshape(atom_count, 2, harmonics, harmonics)
    real_new = product(matrices[:, 0], coeffs[:, 0]) - product(matrices[:, 1], coeffs[:, 1])
    imag_new = product(matrices[:, 0], coeffs[:, 1]) + product(matrices[:, 1], coeffs[:, 0])
    return jnp.stack([real_new, imag_new], axis=1).astype(jnp.bfloat16)


def return_block(template_flat, applied, cos_part, sin_part, chosen):
    atom_count, _, harmonics, band_count = applied.shape
    species_count = chosen.shape[1]
    reordered = jnp.transpose(applied, (2, 0, 1, 3))
    selected = jnp.stack(
        [
            reordered * chosen[:, species_id][None, :, None, None].astype(jnp.bfloat16)
            for species_id in range(species_count)
        ]
    )
    selected = selected.reshape(species_count * harmonics, atom_count * 2 * band_count)
    images = lax.dot_general(
        selected, template_flat, (((0,), (0,)), ((), ())), preferred_element_type=jnp.float32
    )
    images = images.reshape(atom_count, 2, band_count, template_flat.shape[1])
    real_out = jnp.sum(
        cos_part[:, None, :] * images[:, 0] + sin_part[:, None, :] * images[:, 1], axis=0
    )
    imag_out = jnp.sum(
        cos_part[:, None, :] * images[:, 1] - sin_part[:, None, :] * images[:, 0], axis=0
    )
    return jnp.stack([real_out, imag_out])


def per_device(bands_in, template, potential, miller, positions, species, atom_order, reciprocal):
    pw_count = lax.axis_size("pw")
    group_count = lax.axis_size("atom")
    group_id = lax.axis_index("atom")
    slot_dev = potential.shape[0]
    per_group = slot_dev * pw_count
    species_count, harmonics, wave_count = template.shape
    band_count = bands_in.shape[1]
    template_flat = template.reshape(species_count * harmonics, wave_count)
    local_rows = jnp.arange(per_group, dtype=jnp.int32)
    slot_ids = (local_rows // slot_dev * group_count + group_id) * slot_dev + local_rows % slot_dev
    atoms_here = atom_order[slot_ids]
    centres = positions[:, atoms_here]
    kinds = species[atoms_here]
    chosen = (kinds[:, None] == jnp.arange(species_count, dtype=jnp.int32)[None, :]).astype(
        jnp.float32
    )
    miller_real = miller.astype(jnp.float32)
    kinetic = 0.5 * (
        (reciprocal[0] * miller_real[0]) ** 2
        + (reciprocal[1] * miller_real[1]) ** 2
        + (reciprocal[2] * miller_real[2]) ** 2
    )
    cos_all, sin_all = phases(miller_real, centres)
    block_size = math.gcd(per_group, 32)
    block_count = per_group // block_size
    row_width = 2 * harmonics * band_count

    def apply_once(fields):

        def projected(blocknum):
            first_row = blocknum * block_size
            chosen_part = lax.dynamic_slice_in_dim(chosen, first_row, block_size, 0)
            cos_part = lax.dynamic_slice_in_dim(cos_all, first_row, block_size, 0)
            sin_part = lax.dynamic_slice_in_dim(sin_all, first_row, block_size, 0)
            return project_block(template_flat, fields, cos_part, sin_part, chosen_part)

        coeffs = lax.map(projected, jnp.arange(block_count, dtype=jnp.int32)).reshape(
            per_group, row_width
        )
        summed = lax.psum(coeffs, "pw")
        segment = lax.all_gather(potential, "pw", axis=0, tiled=True)
        row_count = segment.shape[0]
        segment_coeffs = summed.reshape(row_count, 2, harmonics, band_count)
        applied = apply_potential(segment, segment_coeffs).reshape(row_count, row_width)
        applied = applied.reshape(per_group, 2, harmonics, band_count)

        def returned(blocknum, summed_up):
            first_row = (blocknum * block_size).astype(jnp.int32)
            chosen_part = lax.dynamic_slice_in_dim(chosen, first_row, block_size, 0)
            applied_part = lax.dynamic_slice_in_dim(applied, first_row, block_size, 0)
            cos_part = lax.dynamic_slice_in_dim(cos_all, first_row, block_size, 0)
            sin_part = lax.dynamic_slice_in_dim(sin_all, first_row, block_size, 0)
            return summed_up + return_block(
                template_flat, applied_part, cos_part, sin_part, chosen_part
            )

        summed_up = lax.fori_loop(
            0, block_count, returned, jnp.zeros((2, band_count, wave_count), jnp.float32)
        )
        return lax.psum(summed_up, "atom") + kinetic[None, None, :] * fields

    applied_once = apply_once(bands_in)
    applied_twice = apply_once(applied_once)
    return (applied_once, applied_twice)


def solution(mesh):
    in_specs = (
        P(None, None, "pw"),
        P(None, None, "pw"),
        P(("pw", "atom"), None),
        P(None, "pw"),
        P(),
        P(),
        P(),
        P(),
    )
    out_specs = (P(None, None, "pw"), P(None, None, "pw"))
    return jax.shard_map(
        per_device, mesh=mesh, in_specs=in_specs, out_specs=out_specs, check_vma=False
    )
```

profile of v0, /device:TPU:1, one launch (start us, length us, event | category | flops | bytes accessed | tf_op | source)
XLA Modules:
  0.0 1698.9 jit_solution(8377880044509035921)
XLA Ops:
  8.7 0.9 copy.40
  9.7 1.4 gather_fusion
  12.1 1.9 gather_fusion.2
  14.0 3.1 fusion.24
  17.4 25.3 %while.48 = (s32[]{:T(128)}, f32[8,32,2,64,8]{3,4,1,0,2:T(8,128)S(1)}, s32[8]{0:T(128)S(1)}, f32[256,2]{0,1:T(2,128)S(1)}, f32[256,512]{1,0:T(8,128)}, /*index=5...) while((s32[]{:T(128)}, ...), condition=%wide.region_1.2_spmd, body=%wide.region_0.1_spmd.sunk | while | flops 68517896 | bytes 4819139 | solution.py:114
  18.6 0.9 constant_dynamic-slice_fusion.22
  21.8 0.9 constant_dynamic-slice_fusion.22
  25.0 0.9 constant_dynamic-slice_fusion.22
  28.1 0.9 constant_dynamic-slice_fusion.22
  31.3 0.9 constant_dynamic-slice_fusion.22
  34.5 0.9 constant_dynamic-slice_fusion.22
  37.6 0.9 constant_dynamic-slice_fusion.22
  42.7 1.3 copy-done.4
  44.9 1.9 add_multiply_fusion.1
  46.9 224.9 %all-gather.3.cloned.1.call-done = bf16[64,4,8192]{2,1,0:T(4,128)(2,1)} async-done(((bf16[1,4,8192]{2,1,0:T(4,128)(2,1)}), bf16[64,4,8192]{2,1,0:T(4,128)(2,1)}) %all-gather.3.cloned.1.call-update) | async-done | bytes 4194320 | tf_op jit(solution)/shard_map/all_gather | solution.py:118
  271.8 13.4 reshape.268
  285.2 601.6 %all-reduce.3.cloned.1.call-done = f32[256,2,64,8]{2,3,0,1:T(8,128)} async-done(((f32[256,2,64,8]{2,3,0,1:T(8,128)}), f32[256,2,64,8]{2,3,0,1:T(8,128)}) %all-reduce.3.cloned.1.call-update) | async-done | bytes 1048592 | tf_op jit(solution)/shard_map/psum | solution.py:117
  886.7 8.6 fusion.6
  895.4 8.6 fusion.7
  904.0 6.6 fusion.21
  910.6 6.6 fusion.20
  917.4 16.8 while.50
  934.2 57.2 %psum.29 = f32[2,8,512]{2,1,0:T(8,128)S(1)} all-reduce(f32[2,8,512]{2,1,0:T(8,128)S(1)} %get-tuple-element.335), channel_id=1, replica_groups=mesh['pw'=64,'atom'=4] {'atom'}, use_global_device_ids=true, to_apply=%region_7.8 | all-reduce | flops 8192 | bytes 65536 | tf_op jit(solution)/shard_map/psum | solution.py:137
  991.6 25.3 %while.49 = (s32[]{:T(128)}, f32[8,32,2,64,8]{3,4,1,0,2:T(8,128)S(1)}, s32[8]{0:T(128)S(1)}, f32[256,2]{0,1:T(2,128)S(1)}, f32[256,512]{1,0:T(8,128)}, /*index=5...) while((s32[]{:T(128)}, ...), condition=%wide.region_9.10_spmd, body=%wide.region_8.9_spmd.sunk | while | flops 68517896 | bytes 4819139 | solution.py:114
  1017.0 1.3 copy-done.3
  1018.3 567.7 %all-reduce.5.cloned.1.call-done = f32[256,2,64,8]{2,3,0,1:T(8,128)} async-done(((f32[256,2,64,8]{2,3,0,1:T(8,128)}), f32[256,2,64,8]{2,3,0,1:T(8,128)}) %all-reduce.5.cloned.1.call-update) | async-done | bytes 1048592 | tf_op jit(solution)/shard_map/psum | solution.py:117
  1586.1 8.6 fusion.4
  1594.7 8.5 fusion.5
  1603.2 8.3 fusion.23
  1611.5 6.6 fusion.22
  1618.4 16.8 while.51
  1635.1 56.6 %psum.31 = f32[2,8,512]{2,1,0:T(8,128)S(1)} all-reduce(f32[2,8,512]{2,1,0:T(8,128)S(1)} %get-tuple-element.337), channel_id=1, replica_groups=mesh['pw'=64,'atom'=4] {'atom'}, use_global_device_ids=true, to_apply=%region_15.16 | all-reduce | flops 8192 | bytes 65536 | tf_op jit(solution)/shard_map/psum | solution.py:137
  (395 shorter events, 70.2 us)
Async XLA Ops:
  7.2 2.5 copy-start
  7.2 10.1 copy-start.8
  7.2 10.1 copy-start.2
  7.2 264.6 %all-gather.3.cloned.1.call-start = ((), (), s32[]{:S(2)}) async-start(), calls=%async_computation.2 | async-start | bytes 4259840 | tf_op jit(solution)/shard_map/all_gather | solution.py:118
  7.9 878.8 %all-reduce.3.cloned.1.call-start = ((), (), s32[]{:S(2)}) async-start(), calls=%async_computation | async-start | bytes 4194304 | tf_op jit(solution)/shard_map/psum | solution.py:117
  17.3 26.9 %copy-start.9 = (f32[3]{0:T(128)S(1)}, f32[3]{0:T(128)}, u32[]{:S(2)}) copy-start(f32[3]{0:T(128)} %param.23) | copy-start | bytes 40
  42.7 1.3 copy-start.4
  44.0 1542.0 %all-reduce.5.cloned.1.call-start = ((), (), s32[]{:S(2)}) async-start(), calls=%async_computation.1 | async-start | bytes 4194304 | tf_op jit(solution)/shard_map/psum | solution.py:117
  886.7 17.3 %copy-start.1 = (bf16[256,2,64,64]{3,2,1,0:T(8,128)(2,1)S(1)}, bf16[256,2,64,64]{3,2,1,0:T(8,128)(2,1)}, u32[]{:S(2)}) copy-start(bf16[256,2,64,64]{3,2,1,0:T(8,128)(2,1)} %reshape.268) | copy-start | bytes 12582916
  895.3 8.6 copy-start.5
  1016.9 1.3 copy-start.3
  1017.0 674.8 %copy-start.7 = (f32[2,8,512]{2,1,0:T(8,128)}, f32[2,8,512]{2,1,0:T(8,128)S(1)}, u32[]{:S(2)}) copy-start(f32[2,8,512]{2,1,0:T(8,128)S(1)} %get-tuple-element.947) | copy-start | bytes 98308
  1586.1 8.6 copy-start.6
  1586.1 25.4 %slice-start = ((s8[8388608]{0:T(1024)(128)(4,1)}), s8[4194304]{0:T(1024)(128)(4,1)S(1)}, s32[]{:S(2)}) async-start(s8[8388608]{0:T(1024)(128)(4,1)} %bitcast.282), calls=%async_computation.3 | async-start | bytes 8388608
  1594.7 16.8 slice-start.1
Sparse Core Ops, SparseCore 0:
  9.8 261.9 all-gather.2
  274.4 612.2 all-reduce.2
  1018.4 567.5 all-reduce.4
where the time goes:
time: 1700 us
  waiting for transfers between devices  1390 us (82%)
  blocking collectives  114 us (7%)
  local copies, waits for them, and re-layouts  73.1 us (4%)
  matrix products  71.7 us (4%)
  other arithmetic  18.1 us (1%)
    psum x2, waiting for transfers between devices, apply_once(): summed = lax.psum(coeffs, 'pw')  1170 us
    all_gather x1, waiting for transfers between devices, apply_once(): segment = lax.all_gather(potential, 'pw', axis=0, tiled=True)  225 us
    psum x2, blocking collectives, apply_once(): return lax.psum(summed_up, 'atom') + kinetic[None, None, :] * fields  114 us
    dot_general x8, matrix products, product(): jnp.einsum('alm,amb->alb', matrices, vectors, precision=lax.Precision.HIG...  62.5 us
  transfers between devices with their start and end apart: 3, of which 3 were waited for; matrix products, arithmetic and copies ran while one was open for 3% of the time, Pallas kernels for 0%

commit v1 on v0

--- a/solution.py
+++ b/solution.py
@@ -115,7 +115,8 @@
             per_group, row_width
         )
         summed = lax.psum(coeffs, "pw")
-        segment = lax.all_gather(potential, "pw", axis=0, tiled=True)
+        repeated = jnp.stack([potential] * lax.axis_size("pw"))
+        segment = jnp.concatenate(lax.all_to_all(repeated, "pw", 0, 0), axis=0)
         row_count = segment.shape[0]
         segment_coeffs = summed.reshape(row_count, 2, harmonics, band_count)
         applied = apply_potential(segment, segment_coeffs).reshape(row_count, row_width)

time: 1700 us -> 1450 us (0.85)
  waiting for transfers between devices: 1390 us -> 1130 us
    all_gather x1 -> x0, waiting for transfers between devices: 225 us -> none  [apply_once(): segment = lax.all_gather(potential, 'pw', axis=0, tiled=True)]
    psum x2, waiting for transfers between devices: 1170 us -> 1070 us  [apply_once(): summed = lax.psum(coeffs, 'pw')]
    all_to_all x0 -> x1, waiting for transfers between devices: none -> 55.9 us  [apply_once(): segment = jnp.concatenate(lax.all_to_all(repeated, 'pw', 0, 0), axis=0)]
where the time goes in v1:
time: 1450 us
  waiting for transfers between devices  1130 us (78%)
  blocking collectives  114 us (8%)
  local copies, waits for them, and re-layouts  76.6 us (5%)
  matrix products  71.8 us (5%)
  other arithmetic  17.4 us (1%)
    psum x2, waiting for transfers between devices, apply_once(): summed = lax.psum(coeffs, 'pw')  1070 us
    psum x2, blocking collectives, apply_once(): return lax.psum(summed_up, 'atom') + kinetic[None, None, :] * fields  114 us
    dot_general x8, matrix products, product(): jnp.einsum('alm,amb->alb', matrices, vectors, precision=lax.Precision.HIG...  62.5 us
    all_to_all x1, waiting for transfers between devices, apply_once(): segment = jnp.concatenate(lax.all_to_all(repeated, 'pw', 0, 0), axis=0)  55.9 us
  transfers between devices with their start and end apart: 3, of which 3 were waited for; matrix products, arithmetic and copies ran while one was open for 3% of the time, Pallas kernels for 0%

profile of v1, /device:TPU:1, one launch (start us, length us, event | category | flops | bytes accessed | tf_op | source)
XLA Modules:
  0.0 1447.9 jit_solution(13912880028599967163)
XLA Ops:
  7.2 4.8 stack.110
  12.0 13.9 all-to-all-start
  26.3 1.4 gather_fusion
  28.7 1.4 gather_fusion.2
  30.1 3.1 fusion.24
  33.4 25.3 %while.48 = (s32[]{:T(128)}, f32[8,32,2,64,8]{3,4,1,0,2:T(8,128)S(1)}, s32[8]{0:T(128)S(1)}, f32[256,2]{0,1:T(2,128)S(1)}, f32[256,512]{1,0:T(8,128)}, /*index=5...) while((s32[]{:T(128)}, ...), condition=%wide.region_1.2_spmd, body=%wide.region_0.1_spmd.sunk | while | flops 68517896 | bytes 4819139 | solution.py:114
  58.8 1.3 copy-done.5
  61.0 1.9 add_multiply_fusion.1
  62.9 55.9 %all-to-all-done = bf16[64,4,8192]{2,1,0:T(4,128)(2,1)} async-done(((bf16[64,4,8192]{2,1,0:T(4,128)(2,1)}), bf16[64,4,8192]{2,1,0:T(4,128)(2,1)}, u32[]{:S(2)}, u32[]{:S(2)}) %all-to-all-start) | async-done | bytes 4194336 | tf_op jit(solution)/shard_map/all_to_all | solution.py:119
  118.9 13.4 reshape.273
  132.3 503.1 %all-reduce.3.cloned.1.call-done = f32[256,2,64,8]{2,3,0,1:T(8,128)} async-done(((f32[256,2,64,8]{2,3,0,1:T(8,128)}), f32[256,2,64,8]{2,3,0,1:T(8,128)}) %all-reduce.3.cloned.1.call-update) | async-done | bytes 1048592 | tf_op jit(solution)/shard_map/psum | solution.py:117
  635.4 8.6 fusion.6
  644.0 8.6 fusion.7
  652.7 6.6 fusion.21
  659.3 6.6 fusion.20
  666.1 16.8 %while.50 = (s32[]{:T(128)}, f32[2,8,512]{2,1,0:T(8,128)S(1)}, f32[256,512]{1,0:T(8,128)}, bf16[256,2,64,8]{2,3,0,1:T(8,128)(2,1)S(1)}, bf16[256,2]{0,1:T(2,128)...) while((s32[]{:T(128)}, f32[2,8,512]{2,1,0:T(8,128)S(1)}, ...), condition=%wide.region_6.7_spmd.clone, body=%wide.region_3.6_spmd.clone.sunk | while | flops 68468744 | bytes 3933881 | solution.py:135
  667.1 0.9 constant_dynamic-slice_fusion.27
  669.2 0.9 constant_dynamic-slice_fusion.27
  671.3 0.9 constant_dynamic-slice_fusion.27
  673.4 0.9 constant_dynamic-slice_fusion.27
  675.5 0.9 constant_dynamic-slice_fusion.27
  677.6 0.9 constant_dynamic-slice_fusion.27
  682.9 57.2 %psum.29 = f32[2,8,512]{2,1,0:T(8,128)S(1)} all-reduce(f32[2,8,512]{2,1,0:T(8,128)S(1)} %get-tuple-element.335), channel_id=1, replica_groups=mesh['pw'=64,'atom'=4] {'atom'}, use_global_device_ids=true, to_apply=%region_7.8 | all-reduce | flops 8192 | bytes 65536 | tf_op jit(solution)/shard_map/psum | solution.py:138
  740.3 25.3 %while.49 = (s32[]{:T(128)}, f32[8,32,2,64,8]{3,4,1,0,2:T(8,128)S(1)}, s32[8]{0:T(128)S(1)}, f32[256,2]{0,1:T(2,128)S(1)}, f32[256,512]{1,0:T(8,128)}, /*index=5...) while((s32[]{:T(128)}, ...), condition=%wide.region_9.10_spmd, body=%wide.region_8.9_spmd.sunk | while | flops 68517896 | bytes 4819139 | solution.py:114
  765.7 1.3 copy-done.4
  767.0 567.8 %all-reduce.5.cloned.1.call-done = f32[256,2,64,8]{2,3,0,1:T(8,128)} async-done(((f32[256,2,64,8]{2,3,0,1:T(8,128)}), f32[256,2,64,8]{2,3,0,1:T(8,128)}) %all-reduce.5.cloned.1.call-update) | async-done | bytes 1048592 | tf_op jit(solution)/shard_map/psum | solution.py:117
  1334.8 8.6 fusion.4
  1343.4 8.5 fusion.5
  1351.9 8.3 fusion.23
  1360.2 6.6 fusion.22
  1367.1 16.8 %while.51 = (s32[]{:T(128)}, f32[2,8,512]{2,1,0:T(8,128)S(1)}, f32[256,512]{1,0:T(8,128)}, bf16[256,2,64,8]{2,3,0,1:T(8,128)(2,1)S(1)}, bf16[256,2]{0,1:T(2,128)...) while((s32[]{:T(128)}, f32[2,8,512]{2,1,0:T(8,128)S(1)}, ...), condition=%wide.region_14.15_spmd.clone, body=%wide.region_11.14_spmd.clone.sunk | while | flops 68468744 | bytes 3933881 | solution.py:135
  1383.9 56.6 %psum.31 = f32[2,8,512]{2,1,0:T(8,128)S(1)} all-reduce(f32[2,8,512]{2,1,0:T(8,128)S(1)} %get-tuple-element.337), channel_id=1, replica_groups=mesh['pw'=64,'atom'=4] {'atom'}, use_global_device_ids=true, to_apply=%region_15.16 | all-reduce | flops 8192 | bytes 65536 | tf_op jit(solution)/shard_map/psum | solution.py:138
  (401 shorter events, 69.9 us)
Async XLA Ops:
  7.2 19.1 %copy-start = (s32[1024]{0:T(1024)S(1)}, s32[1024]{0:T(1024)}, u32[]{:S(2)}) copy-start(s32[1024]{0:T(1024)} %param.22) | copy-start | bytes 12292
  12.0 14.0 copy-start.11
  12.0 14.0 copy-start.10
  12.0 16.7 %copy-start.1 = (s32[1024]{0:T(1024)S(1)}, s32[1024]{0:T(1024)}, u32[]{:S(2)}) copy-start(s32[1024]{0:T(1024)} %param.21) | copy-start | bytes 12292
  12.0 106.9 %all-to-all-start = ((bf16[64,4,8192]{2,1,0:T(4,128)(2,1)}), bf16[64,4,8192]{2,1,0:T(4,128)(2,1)}, u32[]{:S(2)}, u32[]{:S(2)}) async-start(bf16[64,4,8192]{2,1,0:T(4,128)(2,1)} %stack.110), calls=%async_computation | async-start | bytes 8388608 | tf_op jit(solution)/shard_map/all_to_all | solution.py:119
  25.9 7.5 copy-start.3
  25.9 7.5 copy-start.9
  25.9 609.5 %all-reduce.3.cloned.1.call-start = ((), (), s32[]{:S(2)}) async-start(), calls=%async_computation.1 | async-start | bytes 4194304 | tf_op jit(solution)/shard_map/psum | solution.py:117
  33.4 26.9 %copy-start.12 = (f32[3]{0:T(128)S(1)}, f32[3]{0:T(128)}, u32[]{:S(2)}) copy-start(f32[3]{0:T(128)} %param.23) | copy-start | bytes 40
  58.7 1.3 copy-start.5
  60.1 1274.7 %all-reduce.5.cloned.1.call-start = ((), (), s32[]{:S(2)}) async-start(), calls=%async_computation.2 | async-start | bytes 4194304 | tf_op jit(solution)/shard_map/psum | solution.py:117
  635.4 17.3 %copy-start.2 = (bf16[256,2,64,64]{3,2,1,0:T(8,128)(2,1)S(1)}, bf16[256,2,64,64]{3,2,1,0:T(8,128)(2,1)}, u32[]{:S(2)}) copy-start(bf16[256,2,64,64]{3,2,1,0:T(8,128)(2,1)} %reshape.273) | copy-start | bytes 12582916
  644.0 8.6 copy-start.6
  765.6 1.3 copy-start.4
  765.6 674.8 %copy-start.8 = (f32[2,8,512]{2,1,0:T(8,128)}, f32[2,8,512]{2,1,0:T(8,128)S(1)}, u32[]{:S(2)}) copy-start(f32[2,8,512]{2,1,0:T(8,128)S(1)} %get-tuple-element.933) | copy-start | bytes 98308
  1334.8 8.6 copy-start.7
  1334.8 25.4 %slice-start = ((s8[8388608]{0:T(1024)(128)(4,1)}), s8[4194304]{0:T(1024)(128)(4,1)S(1)}, s32[]{:S(2)}) async-start(s8[8388608]{0:T(1024)(128)(4,1)} %bitcast.281), calls=%async_computation.3 | async-start | bytes 8388608
  1343.4 16.8 %slice-start.1 = ((s8[8388608]{0:T(1024)(128)(4,1)}), s8[4194304]{0:T(1024)(128)(4,1)S(1)}, s32[]{:S(2)}) async-start(s8[8388608]{0:T(1024)(128)(4,1)} %bitcast.281), calls=%async_computation.4 | async-start | bytes 8388608
Sparse Core Ops, SparseCore 0:
  60.2 575.1 all-reduce.2
  767.1 567.6 all-reduce.4
